TPU v7x, 32 devices: a whole 2x2x4 slice. The times are simulated.
32 devices in a mesh: section: 2 (over core), seq: 4 (over y, x), tensor: 4 (over z).
Axes of the slice: x: 2, y: 2, z: 4, core: 2. Of those that a mesh axis runs over, the one named last changes fastest.
Arguments:
- tokens: bfloat16 [4096, 1024], P('seq', 'tensor'), may hold values from -6 to 6
- segments: int32 [8, 512], P('seq'), may hold values from 0 to 3, never falling along the last dimension, each value on 1 to 256 neighbouring positions
- cotangent: bfloat16 [4096, 1024], P('seq', 'tensor'), may hold values from -6 to 6
- norm1_gain: bfloat16 [2, 1024], P('section', ('tensor', 'seq')), may hold values from 0.5 to 1.5
- norm1_bias: bfloat16 [2, 1024], P('section', ('tensor', 'seq')), may hold values from -3 to 3
- qkv_weight: bfloat16 [2, 1024, 16, 192], P('section', 'seq', 'tensor'), may hold values from -0.1875 to 0.1875
- qv_bias: bfloat16 [2, 16, 128], P('section', 'tensor', 'seq'), may hold values from -4 to 4
- out_weight: bfloat16 [2, 16, 64, 1024], P('section', 'tensor', None, 'seq'), may hold values from -0.75 to 0.75
- out_bias: bfloat16 [2, 1024], P('section', ('tensor', 'seq')), may hold values from -3 to 3
- norm2_gain: bfloat16 [2, 1024], P('section', ('tensor', 'seq')), may hold values from 0.5 to 1.5
- norm2_bias: bfloat16 [2, 1024], P('section', ('tensor', 'seq')), may hold values from -3 to 3
- up_weight: bfloat16 [2, 1024, 4096], P('section', 'seq', 'tensor'), may hold values from -0.1875 to 0.1875
- up_bias: bfloat16 [2, 4096], P('section', ('tensor', 'seq')), may hold values from -4 to 4
- down_weight: bfloat16 [2, 4096, 1024], P('section', 'tensor', 'seq'), may hold values from -0.09375 to 0.09375
- down_bias: bfloat16 [2, 1024], P('section', ('tensor', 'seq')), may hold values from -3 to 3
Outputs:
- section_out: bfloat16 [2, 4096, 1024], P('section', 'seq', 'tensor')
- input_grad: bfloat16 [2, 4096, 1024], P('section', 'seq', 'tensor')
- grad_norm1_gain: float32 [2, 1024], P('section', ('tensor', 'seq'))
- grad_norm1_bias: float32 [2, 1024], P('section', ('tensor', 'seq'))
- grad_qkv_weight: float32 [2, 1024, 16, 192], P('section', 'seq', 'tensor')
- grad_qv_bias: float32 [2, 16, 128], P('section', 'tensor', 'seq')
- grad_out_weight: float32 [2, 16, 64, 1024], P('section', 'tensor', None, 'seq')
- grad_out_bias: float32 [2, 1024], P('section', ('tensor', 'seq'))
- grad_norm2_gain: float32 [2, 1024], P('section', ('tensor', 'seq'))
- grad_norm2_bias: float32 [2, 1024], P('section', ('tensor', 'seq'))
- grad_up_weight: float32 [2, 1024, 4096], P('section', 'seq', 'tensor')
- grad_up_bias: float32 [2, 4096], P('section', ('tensor', 'seq'))
- grad_down_weight: float32 [2, 4096, 1024], P('section', 'tensor', 'seq')
- grad_down_bias: float32 [2, 1024], P('section', ('tensor', 'seq'))
Inputs may be any that keep to these rules, and one draw needn't show every extreme that they name: `segments`: along each sequence the document numbers never fall; every document holds 1 to 256 positions.
All inputs are finite; a program needn't handle non-finite values.
Results may differ from a plain program's by a relative error of at most 0.02.
Values may be sent and summed in bfloat16 or wider, within the bound.
A program may use at most 192 MiB of HBM per device.

v0:
```python
import math
import jax
import jax.numpy as jnp
from jax import lax
from jax.sharding import PartitionSpec as P

D = 1024
MB = 2
epsilon = 1e-05
floor_value = -1e30


def passed_along(shard, axis, by):
    devices = lax.axis_size(axis)
    pairs = [(i, i + by) for i in range(devices) if 0 <= i + by < devices]
    return lax.ppermute(shard, axis, pairs)


def row_totals(first, second):
    return lax.psum((jnp.sum(first, axis=1), jnp.sum(second, axis=1)), "tensor")


def norm_forward(rows, gain, shift):
    total, square = row_totals(rows, rows * rows)
    average = total / D
    variance = square / D - average * average
    scale = lax.rsqrt(variance + epsilon)
    centred = (rows - average[:, None]) * scale[:, None]
    return (centred, scale, centred * gain + shift)


def norm_backward(grad, centred, scale, gain):
    scaled = grad * gain
    total, along = row_totals(scaled, scaled * centred)
    return scale[:, None] * (scaled - total[:, None] / D - centred * along[:, None] / D)


def full_rows(piece):
    return lax.all_gather(piece, "tensor", axis=1, tiled=True)


def head_sums(partial_rows):
    return lax.psum_scatter(
        partial_rows.astype(jnp.bfloat16), "tensor", scatter_dimension=1, tiled=True
    ).astype(jnp.float32)


def grad_full(piece):
    return lax.all_gather(piece, "tensor", axis=1, tiled=True)


def back_sums(partial_rows):
    return lax.psum_scatter(
        partial_rows.astype(jnp.bfloat16), "tensor", scatter_dimension=1, tiled=True
    ).astype(jnp.float32)


def allowed_mask(segment):
    length = segment.shape[1]
    place = lax.broadcasted_iota(jnp.int32, (length, length), 0)
    other = lax.broadcasted_iota(jnp.int32, (length, length), 1)
    same = segment[:, :, None] == segment[:, None, :]
    return (same & (other <= place)[None])[:, None]


def attention_scores(query, keys, segment):
    head_dim = query.shape[-1]
    factor = 1.0 / math.sqrt(head_dim)
    scores = jnp.einsum("sqhe,skhe->shqk", query, keys, preferred_element_type=jnp.float32) * factor
    return (jnp.where(allowed_mask(segment), scores, floor_value), factor)


def forward(rows, segment, weights):
    gain1, bias1, w_qkv, b_qv, w_out, b_out, gain2, bias2, w_up, b_up, w_down, b_down = weights
    count_rows = rows.shape[0]
    heads = w_qkv.shape[1]
    head_dim = w_qkv.shape[2] // 3
    shape4 = (segment.shape[0], segment.shape[1], heads, head_dim)
    centred1, scale1, normed1 = norm_forward(rows, gain1, bias1)
    normed_whole = full_rows(normed1.astype(jnp.bfloat16))
    mixed = jnp.einsum("rd,dhe->rhe", normed_whole, w_qkv, preferred_element_type=jnp.float32)
    query = (mixed[..., :head_dim] + b_qv[:, :head_dim]).astype(jnp.bfloat16).reshape(shape4)
    keys = mixed[..., head_dim : 2 * head_dim].astype(jnp.bfloat16).reshape(shape4)
    values = (mixed[..., 2 * head_dim :] + b_qv[:, head_dim:]).astype(jnp.bfloat16).reshape(shape4)
    masked, factor = attention_scores(query, keys, segment)
    highest_score = jnp.max(masked, axis=-1, keepdims=True)
    raised = jnp.exp(masked - highest_score)
    total = jnp.sum(raised, axis=-1, keepdims=True)
    chance = (raised / total).astype(jnp.bfloat16)
    logsum = highest_score + jnp.log(total)
    context = jnp.einsum("shqk,skhe->sqhe", chance, values, preferred_element_type=jnp.float32)
    context = context.reshape(count_rows, heads * head_dim).astype(jnp.bfloat16)
    attn_part = jnp.dot(
        context, w_out.reshape(heads * head_dim, w_out.shape[2]), preferred_element_type=jnp.float32
    )
    hidden = rows + (head_sums(attn_part) + b_out)
    centred2, scale2, normed2 = norm_forward(hidden, gain2, bias2)
    normed2_whole = full_rows(normed2.astype(jnp.bfloat16))
    upper = jnp.dot(normed2_whole, w_up, preferred_element_type=jnp.float32) + b_up
    active = jax.nn.gelu(upper, approximate=True).astype(jnp.bfloat16)
    branch = head_sums(jnp.dot(active, w_down, preferred_element_type=jnp.float32)) + b_down
    output = (hidden + branch).astype(jnp.bfloat16)
    kept = (
        centred1,
        scale1,
        normed_whole,
        query,
        keys,
        values,
        logsum,
        context,
        centred2,
        scale2,
        normed2_whole,
        upper,
        active,
    )
    return (output, kept)


def gelu_value(upper):
    return jax.nn.gelu(upper, approximate=True)


def backward(grad_out, segment, weights, kept):
    gain1, bias1, w_qkv, b_qv, w_out, b_out, gain2, bias2, w_up, b_up, w_down, b_down = weights
    (
        centred1,
        scale1,
        normed_whole,
        query,
        keys,
        values,
        logsum,
        context,
        centred2,
        scale2,
        normed2_whole,
        upper,
        active,
    ) = kept
    count_rows = grad_out.shape[0]
    heads = w_qkv.shape[1]
    head_dim = w_qkv.shape[2] // 3
    shape4 = query.shape
    grad_branch = grad_out.astype(jnp.bfloat16)
    branch_whole = grad_full(grad_branch)
    grad_down = jnp.einsum("rf,rd->fd", active, branch_whole, preferred_element_type=jnp.float32)
    grad_active = jnp.einsum("rd,fd->rf", branch_whole, w_down, preferred_element_type=jnp.float32)
    grad_upper = jax.vjp(gelu_value, upper)[1](grad_active)[0].astype(jnp.bfloat16)
    grad_up = jnp.einsum("rd,rf->df", normed2_whole, grad_upper, preferred_element_type=jnp.float32)
    grad_normed2 = back_sums(
        jnp.einsum("rf,df->rd", grad_upper, w_up, preferred_element_type=jnp.float32)
    )
    grad_hidden = grad_out + norm_backward(grad_normed2, centred2, scale2, gain2)
    grad_attn = grad_hidden.astype(jnp.bfloat16)
    attn_whole = grad_full(grad_attn)
    out_matrix = w_out.reshape(heads * head_dim, w_out.shape[2])
    grad_out_w = jnp.einsum("rc,rd->cd", context, attn_whole, preferred_element_type=jnp.float32)
    grad_context = jnp.einsum(
        "rd,cd->rc", attn_whole, out_matrix, preferred_element_type=jnp.float32
    )
    grad_context = grad_context.astype(jnp.bfloat16).reshape(shape4)
    masked, factor = attention_scores(query, keys, segment)
    chance_full = jnp.exp(masked - logsum)
    chance = chance_full.astype(jnp.bfloat16)
    grad_chance = jnp.einsum(
        "sqhe,skhe->shqk", grad_context, values, preferred_element_type=jnp.float32
    )
    delta = jnp.sum(grad_chance * chance_full, axis=-1, keepdims=True)
    grad_scores = (chance_full * (grad_chance - delta)).astype(jnp.bfloat16)
    grad_query = (
        jnp.einsum("shqk,skhe->sqhe", grad_scores, keys, preferred_element_type=jnp.float32)
        * factor
    ).astype(jnp.bfloat16)
    grad_keys = (
        jnp.einsum("shqk,sqhe->skhe", grad_scores, query, preferred_element_type=jnp.float32)
        * factor
    ).astype(jnp.bfloat16)
    grad_values = jnp.einsum(
        "shqk,sqhe->skhe", chance, grad_context, preferred_element_type=jnp.float32
    ).astype(jnp.bfloat16)
    grad_mixed = jnp.concatenate([grad_query, grad_keys, grad_values], axis=-1).reshape(
        count_rows, heads, 3 * head_dim
    )
    grad_qkv = jnp.einsum(
        "rd,rhe->dhe", normed_whole, grad_mixed, preferred_element_type=jnp.float32
    )
    grad_qv = jnp.concatenate(
        [
            jnp.sum(grad_query.astype(jnp.float32), axis=(0, 1)),
            jnp.sum(grad_values.astype(jnp.float32), axis=(0, 1)),
        ],
        axis=-1,
    )
    grad_normed1 = back_sums(
        jnp.einsum("rhe,dhe->rd", grad_mixed, w_qkv, preferred_element_type=jnp.float32)
    )
    grad_rows_total = grad_hidden + norm_backward(grad_normed1, centred1, scale1, gain1)
    grads = (
        jnp.sum(grad_normed1 * centred1, axis=0),
        jnp.sum(grad_normed1, axis=0),
        grad_qkv,
        grad_qv,
        grad_out_w.reshape(w_out.shape),
        jnp.sum(grad_attn.astype(jnp.float32), axis=0),
        jnp.sum(grad_normed2 * centred2, axis=0),
        jnp.sum(grad_normed2, axis=0),
        grad_up,
        jnp.sum(grad_upper.astype(jnp.float32), axis=0),
        grad_down,
        jnp.sum(grad_branch.astype(jnp.float32), axis=0),
    )
    return (grad_rows_total.astype(jnp.bfloat16), grads)


def body(
    tokens,
    segments,
    cotangent,
    norm1_gain,
    norm1_bias,
    qkv_weight,
    qv_bias,
    out_weight,
    out_bias,
    norm2_gain,
    norm2_bias,
    up_weight,
    up_bias,
    down_weight,
    down_bias,
):
    section = lax.axis_index("section")
    first_section = section == 0
    gathered = (
        lax.all_gather(norm1_gain[0], "seq", axis=0, tiled=True),
        lax.all_gather(norm1_bias[0], "seq", axis=0, tiled=True),
        lax.all_gather(qkv_weight[0], "seq", axis=0, tiled=True),
        lax.all_gather(qv_bias[0], "seq", axis=1, tiled=True),
        lax.all_gather(out_weight[0], "seq", axis=2, tiled=True),
        lax.all_gather(out_bias[0], "seq", axis=0, tiled=True),
        lax.all_gather(norm2_gain[0], "seq", axis=0, tiled=True),
        lax.all_gather(norm2_bias[0], "seq", axis=0, tiled=True),
        lax.all_gather(up_weight[0], "seq", axis=0, tiled=True),
        lax.all_gather(up_bias[0], "seq", axis=0, tiled=True),
        lax.all_gather(down_weight[0], "seq", axis=1, tiled=True),
        lax.all_gather(down_bias[0], "seq", axis=0, tiled=True),
    )
    weights = (
        gathered[0].astype(jnp.float32),
        gathered[1].astype(jnp.float32),
        gathered[2],
        gathered[3].astype(jnp.float32),
        gathered[4],
        gathered[5].astype(jnp.float32),
        gathered[6].astype(jnp.float32),
        gathered[7].astype(jnp.float32),
        gathered[8],
        gathered[9].astype(jnp.float32),
        gathered[10],
        gathered[11].astype(jnp.float32),
    )
    rows_batch = tokens.shape[0] // MB
    seqs_batch = segments.shape[0] // MB
    width_local = tokens.shape[1]
    received = jnp.zeros((rows_batch, width_local), jnp.bfloat16)
    outputs = jnp.zeros(tokens.shape, jnp.bfloat16)
    stash = []
    for tick in range(MB + 1):
        own = min(tick, MB - 1)
        batch = tick - section
        valid = (batch >= 0) & (batch < MB)
        placed = jnp.clip(batch, 0, MB - 1)
        entry = jnp.where(
            first_section, tokens[own * rows_batch : (own + 1) * rows_batch], received
        )
        segment = lax.dynamic_slice_in_dim(segments, placed * seqs_batch, seqs_batch, 0)
        result, kept = forward(entry.astype(jnp.float32), segment, weights)
        stash.append((entry, segment))
        current = lax.dynamic_slice_in_dim(outputs, placed * rows_batch, rows_batch, 0)
        outputs = lax.dynamic_update_slice_in_dim(
            outputs, jnp.where(valid, result, current), placed * rows_batch, 0
        )
        if tick < MB:
            received = passed_along(result, "section", 1)
    totals = jax.tree.map(lambda item: jnp.zeros(item.shape, jnp.float32), gathered)
    returned = jnp.zeros((rows_batch, width_local), jnp.bfloat16)
    input_grads = jnp.zeros(tokens.shape, jnp.bfloat16)
    for tick in range(MB + 1):
        own = min(tick, MB - 1)
        batch = tick - (1 - section)
        valid = (batch >= 0) & (batch < MB)
        placed = jnp.clip(batch, 0, MB - 1)
        grad_in = jnp.where(
            first_section, returned, cotangent[own * rows_batch : (own + 1) * rows_batch]
        ).astype(jnp.float32)
        earlier = stash[max(tick - 1, 0)]
        later = stash[min(tick + 1, MB)]
        picked = jax.tree.map(
            lambda left, right: jnp.where(first_section, left, right), earlier, later
        )
        entry = picked[0]
        segment = picked[1]
        kept = forward(entry.astype(jnp.float32), segment, weights)[1]
        grad_rows_out, grads = backward(grad_in, segment, weights, kept)
        totals = jax.tree.map(lambda acc, new: acc + jnp.where(valid, new, 0.0), totals, grads)
        current = lax.dynamic_slice_in_dim(input_grads, placed * rows_batch, rows_batch, 0)
        input_grads = lax.dynamic_update_slice_in_dim(
            input_grads, jnp.where(valid, grad_rows_out, current), placed * rows_batch, 0
        )
        if tick < MB:
            returned = passed_along(grad_rows_out, "section", -1)
    reduced = (
        lax.psum_scatter(
            totals[0].astype(jnp.bfloat16), "seq", scatter_dimension=0, tiled=True
        ).astype(jnp.float32),
        lax.psum_scatter(
            totals[1].astype(jnp.bfloat16), "seq", scatter_dimension=0, tiled=True
        ).astype(jnp.float32),
        lax.psum_scatter(
            totals[2].astype(jnp.bfloat16), "seq", scatter_dimension=0, tiled=True
        ).astype(jnp.float32),
        lax.psum_scatter(
            totals[3].astype(jnp.bfloat16), "seq", scatter_dimension=1, tiled=True
        ).astype(jnp.float32),
        lax.psum_scatter(
            totals[4].astype(jnp.bfloat16), "seq", scatter_dimension=2, tiled=True
        ).astype(jnp.float32),
        lax.psum_scatter(
            totals[5].astype(jnp.bfloat16), "seq", scatter_dimension=0, tiled=True
        ).astype(jnp.float32),
        lax.psum_scatter(
            totals[6].astype(jnp.bfloat16), "seq", scatter_dimension=0, tiled=True
        ).astype(jnp.float32),
        lax.psum_scatter(
            totals[7].astype(jnp.bfloat16), "seq", scatter_dimension=0, tiled=True
        ).astype(jnp.float32),
        lax.psum_scatter(
            totals[8].astype(jnp.bfloat16), "seq", scatter_dimension=0, tiled=True
        ).astype(jnp.float32),
        lax.psum_scatter(
            totals[9].astype(jnp.bfloat16), "seq", scatter_dimension=0, tiled=True
        ).astype(jnp.float32),
        lax.psum_scatter(
            totals[10].astype(jnp.bfloat16), "seq", scatter_dimension=1, tiled=True
        ).astype(jnp.float32),
        lax.psum_scatter(
            totals[11].astype(jnp.bfloat16), "seq", scatter_dimension=0, tiled=True
        ).astype(jnp.float32),
    )
    return (outputs[None], input_grads[None]) + tuple((item[None] for item in reduced))


def solution(mesh):
    return jax.shard_map(
        body,
        mesh=mesh,
        in_specs=(
            P("seq", "tensor"),
            P("seq", None),
            P("seq", "tensor"),
            P("section", ("tensor", "seq")),
            P("section", ("tensor", "seq")),
            P("section", "seq", "tensor", None),
            P("section", "tensor", "seq"),
            P("section", "tensor", None, "seq"),
            P("section", ("tensor", "seq")),
            P("section", ("tensor", "seq")),
            P("section", ("tensor", "seq")),
            P("section", "seq", "tensor"),
            P("section", ("tensor", "seq")),
            P("section", "tensor", "seq"),
            P("section", ("tensor", "seq")),
        ),
        out_specs=(
            P("section", "seq", "tensor"),
            P("section", "seq", "tensor"),
            P("section", ("tensor", "seq")),
            P("section", ("tensor", "seq")),
            P("section", "seq", "tensor", None),
            P("section", "tensor", "seq"),
            P("section", "tensor", None, "seq"),
            P("section", ("tensor", "seq")),
            P("section", ("tensor", "seq")),
            P("section", ("tensor", "seq")),
            P("section", "seq", "tensor"),
            P("section", ("tensor", "seq")),
            P("section", "tensor", "seq"),
            P("section", ("tensor", "seq")),
        ),
        check_vma=False,
    )
```

profile of v0, /device:TPU:0, one launch (start us, length us, event | category | flops | bytes accessed | tf_op | source)
XLA Modules:
  0.0 1450.4 jit_solution(4128099430230138480)
XLA Ops:
  67.1 30.9 %all-gather.70.cloned.1.call-done = bf16[1,1024,4,192]{1,3,2,0:T(8,128)(2,1)} async-done(((bf16[1,256,4,192]{1,3,2,0:T(8,128)(2,1)}), bf16[1,1024,4,192]{1,3,2,0:T(8,128)(2,1)}) %all-gather.70.cloned.1.call-update) | async-done | bytes 1572880 | tf_op jit(solution)/shard_map/all_gather | solution.py:239
  109.8 26.2 %reduce-scatter.23.cloned.1.call-done = bf16[512,256]{1,0:T(8,128)(2,1)} async-done(((bf16[512,1024]{1,0:T(8,128)(2,1)}), bf16[512,256]{1,0:T(8,128)(2,1)}) %reduce-scatter.23.cloned.1.call-update) | async-done | bytes 262160 | tf_op jit(solution)/shard_map/reduce_scatter | solution.py:43
  171.2 36.9 %all-gather.72.cloned.1.call-done = bf16[1,1024,1024]{2,1,0:T(8,128)(2,1)} async-done(((bf16[1,256,1024]{2,1,0:T(8,128)(2,1)}), bf16[1,1024,1024]{2,1,0:T(8,128)(2,1)}) %all-gather.72.cloned.1.call-update) | async-done | bytes 2097168 | tf_op jit(solution)/shard_map/all_gather | solution.py:245
  208.1 31.9 %all-gather.36.cloned.1.call-done = bf16[512,1024]{1,0:T(8,128)(2,1)} async-done(((bf16[512,256]{1,0:T(8,128)(2,1)}), bf16[512,1024]{1,0:T(8,128)(2,1)}) %all-gather.36.cloned.1.call-update) | async-done | bytes 1048592 | tf_op jit(solution)/shard_map/all_gather | solution.py:39
  246.3 25.7 %reduce-scatter.25.cloned.1.call-done = bf16[512,256]{1,0:T(8,128)(2,1)} async-done(((bf16[512,1024]{1,0:T(8,128)(2,1)}), bf16[512,256]{1,0:T(8,128)(2,1)}) %reduce-scatter.25.cloned.1.call-update) | async-done | bytes 262160 | tf_op jit(solution)/shard_map/reduce_scatter | solution.py:43
  286.7 28.2 %all-gather.46.cloned.1.call-done = bf16[512,1024]{1,0:T(8,128)(2,1)} async-done(((bf16[512,256]{1,0:T(8,128)(2,1)}), bf16[512,1024]{1,0:T(8,128)(2,1)}) %all-gather.46.cloned.1.call-update) | async-done | bytes 1048592 | tf_op jit(solution)/shard_map/all_gather | solution.py:39
  323.9 25.5 %reduce-scatter.35.cloned.1.call-done = bf16[512,256]{1,0:T(8,128)(2,1)} async-done(((bf16[512,1024]{1,0:T(8,128)(2,1)}), bf16[512,256]{1,0:T(8,128)(2,1)}) %reduce-scatter.35.cloned.1.call-update) | async-done | bytes 262160 | tf_op jit(solution)/shard_map/reduce_scatter | solution.py:43
  364.5 25.2 %all-gather.38.cloned.1.call-done = bf16[512,1024]{1,0:T(8,128)(2,1)} async-done(((bf16[512,256]{1,0:T(8,128)(2,1)}), bf16[512,1024]{1,0:T(8,128)(2,1)}) %all-gather.38.cloned.1.call-update) | async-done | bytes 1048592 | tf_op jit(solution)/shard_map/all_gather | solution.py:39
  424.6 25.8 %all-gather.48.cloned.1.call-done = bf16[512,1024]{1,0:T(8,128)(2,1)} async-done(((bf16[512,256]{1,0:T(8,128)(2,1)}), bf16[512,1024]{1,0:T(8,128)(2,1)}) %all-gather.48.cloned.1.call-update) | async-done | bytes 1048592 | tf_op jit(solution)/shard_map/all_gather | solution.py:49
  478.9 28.6 %reduce-scatter.37.cloned.1.call-done = bf16[512,256]{1,0:T(8,128)(2,1)} async-done(((bf16[512,1024]{1,0:T(8,128)(2,1)}), bf16[512,256]{1,0:T(8,128)(2,1)}) %reduce-scatter.37.cloned.1.call-update) | async-done | bytes 262160 | tf_op jit(solution)/shard_map/reduce_scatter | solution.py:53
  520.8 28.8 %all-gather.40.cloned.1.call-done = bf16[512,1024]{1,0:T(8,128)(2,1)} async-done(((bf16[512,256]{1,0:T(8,128)(2,1)}), bf16[512,1024]{1,0:T(8,128)(2,1)}) %all-gather.40.cloned.1.call-update) | async-done | bytes 1048592 | tf_op jit(solution)/shard_map/all_gather | solution.py:39
  555.7 25.7 %reduce-scatter.29.cloned.1.call-done = bf16[512,256]{1,0:T(8,128)(2,1)} async-done(((bf16[512,1024]{1,0:T(8,128)(2,1)}), bf16[512,256]{1,0:T(8,128)(2,1)}) %reduce-scatter.29.cloned.1.call-update) | async-done | bytes 262160 | tf_op jit(solution)/shard_map/reduce_scatter | solution.py:43
  597.1 28.5 %all-gather.52.cloned.1.call-done = bf16[512,1024]{1,0:T(8,128)(2,1)} async-done(((bf16[512,256]{1,0:T(8,128)(2,1)}), bf16[512,1024]{1,0:T(8,128)(2,1)}) %all-gather.52.cloned.1.call-update) | async-done | bytes 1048592 | tf_op jit(solution)/shard_map/all_gather | solution.py:49
  637.4 25.7 %reduce-scatter.39.cloned.1.call-done = bf16[512,256]{1,0:T(8,128)(2,1)} async-done(((bf16[512,1024]{1,0:T(8,128)(2,1)}), bf16[512,256]{1,0:T(8,128)(2,1)}) %reduce-scatter.39.cloned.1.call-update) | async-done | bytes 262160 | tf_op jit(solution)/shard_map/reduce_scatter | solution.py:53
  666.0 28.4 %all-gather.54.cloned.1.call-done = bf16[512,1024]{1,0:T(8,128)(2,1)} async-done(((bf16[512,256]{1,0:T(8,128)(2,1)}), bf16[512,1024]{1,0:T(8,128)(2,1)}) %all-gather.54.cloned.1.call-update) | async-done | bytes 1048592 | tf_op jit(solution)/shard_map/all_gather | solution.py:39
  702.5 25.7 %reduce-scatter.41.cloned.1.call-done = bf16[512,256]{1,0:T(8,128)(2,1)} async-done(((bf16[512,1024]{1,0:T(8,128)(2,1)}), bf16[512,256]{1,0:T(8,128)(2,1)}) %reduce-scatter.41.cloned.1.call-update) | async-done | bytes 262160 | tf_op jit(solution)/shard_map/reduce_scatter | solution.py:43
  754.9 19.9 %all-gather.62.cloned.1.call-done = bf16[512,1024]{1,0:T(8,128)(2,1)} async-done(((bf16[512,256]{1,0:T(8,128)(2,1)}), bf16[512,1024]{1,0:T(8,128)(2,1)}) %all-gather.62.cloned.1.call-update) | async-done | bytes 1048592 | tf_op jit(solution)/shard_map/all_gather | solution.py:39
  782.9 22.3 %all-gather.58.cloned.1.call-done = bf16[512,1024]{1,0:T(8,128)(2,1)} async-done(((bf16[512,256]{1,0:T(8,128)(2,1)}), bf16[512,1024]{1,0:T(8,128)(2,1)}) %all-gather.58.cloned.1.call-update) | async-done | bytes 1048592 | tf_op jit(solution)/shard_map/all_gather | solution.py:39
  809.7 25.8 %all-gather.56.cloned.1.call-done = bf16[512,1024]{1,0:T(8,128)(2,1)} async-done(((bf16[512,256]{1,0:T(8,128)(2,1)}), bf16[512,1024]{1,0:T(8,128)(2,1)}) %all-gather.56.cloned.1.call-update) | async-done | bytes 1048592 | tf_op jit(solution)/shard_map/all_gather | solution.py:49
  863.9 28.7 %reduce-scatter.43.cloned.1.call-done = bf16[512,256]{1,0:T(8,128)(2,1)} async-done(((bf16[512,1024]{1,0:T(8,128)(2,1)}), bf16[512,256]{1,0:T(8,128)(2,1)}) %reduce-scatter.43.cloned.1.call-update) | async-done | bytes 262160 | tf_op jit(solution)/shard_map/reduce_scatter | solution.py:53
  907.1 28.3 %all-gather.60.cloned.1.call-done = bf16[512,1024]{1,0:T(8,128)(2,1)} async-done(((bf16[512,256]{1,0:T(8,128)(2,1)}), bf16[512,1024]{1,0:T(8,128)(2,1)}) %all-gather.60.cloned.1.call-update) | async-done | bytes 1048592 | tf_op jit(solution)/shard_map/all_gather | solution.py:49
  947.3 25.7 %reduce-scatter.45.cloned.1.call-done = bf16[512,256]{1,0:T(8,128)(2,1)} async-done(((bf16[512,1024]{1,0:T(8,128)(2,1)}), bf16[512,256]{1,0:T(8,128)(2,1)}) %reduce-scatter.45.cloned.1.call-update) | async-done | bytes 262160 | tf_op jit(solution)/shard_map/reduce_scatter | solution.py:53
  1001.1 20.1 %all-gather.42.cloned.1.call-done = bf16[512,1024]{1,0:T(8,128)(2,1)} async-done(((bf16[512,256]{1,0:T(8,128)(2,1)}), bf16[512,1024]{1,0:T(8,128)(2,1)}) %all-gather.42.cloned.1.call-update) | async-done | bytes 1048592 | tf_op jit(solution)/shard_map/all_gather | solution.py:39
  1056.1 25.2 %all-gather.64.cloned.1.call-done = bf16[512,1024]{1,0:T(8,128)(2,1)} async-done(((bf16[512,256]{1,0:T(8,128)(2,1)}), bf16[512,1024]{1,0:T(8,128)(2,1)}) %all-gather.64.cloned.1.call-update) | async-done | bytes 1048592 | tf_op jit(solution)/shard_map/all_gather | solution.py:49
  1088.8 20.9 %reduce-scatter.31.cloned.1.call-done = bf16[512,256]{1,0:T(8,128)(2,1)} async-done(((bf16[512,1024]{1,0:T(8,128)(2,1)}), bf16[512,256]{1,0:T(8,128)(2,1)}) %reduce-scatter.31.cloned.1.call-update) | async-done | bytes 262160 | tf_op jit(solution)/shard_map/reduce_scatter | solution.py:43
  1109.7 28.7 %reduce-scatter.49.cloned.1.call-done = bf16[512,256]{1,0:T(8,128)(2,1)} async-done(((bf16[512,1024]{1,0:T(8,128)(2,1)}), bf16[512,256]{1,0:T(8,128)(2,1)}) %reduce-scatter.49.cloned.1.call-update) | async-done | bytes 262160 | tf_op jit(solution)/shard_map/reduce_scatter | solution.py:53
  1151.4 28.8 %all-gather.68.cloned.1.call-done = bf16[512,1024]{1,0:T(8,128)(2,1)} async-done(((bf16[512,256]{1,0:T(8,128)(2,1)}), bf16[512,1024]{1,0:T(8,128)(2,1)}) %all-gather.68.cloned.1.call-update) | async-done | bytes 1048592 | tf_op jit(solution)/shard_map/all_gather | solution.py:49
  1257.0 24.2 %reduce-scatter.57.cloned.1.call-done = bf16[256,1024]{1,0:T(8,128)(2,1)} async-done(((bf16[1024,1024]{1,0:T(8,128)(2,1)}), bf16[256,1024]{1,0:T(8,128)(2,1)}) %reduce-scatter.57.cloned.1.call-update) | async-done | bytes 524304 | tf_op jit(solution)/shard_map/reduce_scatter | solution.py:339
  1283.3 29.8 %all-gather.44.cloned.1.call-done = bf16[512,1024]{1,0:T(8,128)(2,1)} async-done(((bf16[512,256]{1,0:T(8,128)(2,1)}), bf16[512,1024]{1,0:T(8,128)(2,1)}) %all-gather.44.cloned.1.call-update) | async-done | bytes 1048592 | tf_op jit(solution)/shard_map/all_gather | solution.py:39
  1319.2 30.4 %reduce-scatter.59.cloned.1.call-done = bf16[1024,256]{1,0:T(8,128)(2,1)} async-done(((bf16[1024,1024]{1,0:T(8,128)(2,1)}), bf16[1024,256]{1,0:T(8,128)(2,1)}) %reduce-scatter.59.cloned.1.call-update) | async-done | bytes 524304 | tf_op jit(solution)/shard_map/reduce_scatter | solution.py:345
  1351.7 25.7 %reduce-scatter.55.cloned.1.call-done = bf16[4,64,256]{2,1,0:T(8,128)(2,1)} async-done(((bf16[4,64,1024]{2,1,0:T(8,128)(2,1)}), bf16[4,64,256]{2,1,0:T(8,128)(2,1)}) %reduce-scatter.55.cloned.1.call-update) | async-done | bytes 131088 | tf_op jit(solution)/shard_map/reduce_scatter | solution.py:327
  1413.5 27.7 %reduce-scatter.33.cloned.1.call-done = bf16[512,256]{1,0:T(8,128)(2,1)} async-done(((bf16[512,1024]{1,0:T(8,128)(2,1)}), bf16[512,256]{1,0:T(8,128)(2,1)}) %reduce-scatter.33.cloned.1.call-update) | async-done | bytes 262160 | tf_op jit(solution)/shard_map/reduce_scatter | solution.py:43
  (513 shorter events, 572.1 us)
Async XLA Ops:
  41.5 94.4 %reduce-scatter.23.cloned.1.call-start = ((), (), s32[]{:S(2)}) async-start(), calls=%async_computation.21 | async-start | bytes 1310720 | tf_op jit(solution)/shard_map/reduce_scatter | solution.py:43
  109.1 99.0 %all-gather.72.cloned.1.call-start = ((), (), s32[]{:S(2)}) async-start(), calls=%async_computation.58 | async-start | bytes 2621440 | tf_op jit(solution)/shard_map/all_gather | solution.py:245
  109.7 130.4 %all-gather.36.cloned.1.call-start = ((), (), s32[]{:S(2)}) async-start(), calls=%async_computation.22 | async-start | bytes 1310720 | tf_op jit(solution)/shard_map/all_gather | solution.py:39
  148.3 123.6 %reduce-scatter.25.cloned.1.call-start = ((), (), s32[]{:S(2)}) async-start(), calls=%async_computation.23 | async-start | bytes 1310720 | tf_op jit(solution)/shard_map/reduce_scatter | solution.py:43
  246.2 68.7 %all-gather.46.cloned.1.call-start = ((), (), s32[]{:S(2)}) async-start(), calls=%async_computation.32 | async-start | bytes 1310720 | tf_op jit(solution)/shard_map/all_gather | solution.py:39
  286.2 63.2 %reduce-scatter.35.cloned.1.call-start = ((), (), s32[]{:S(2)}) async-start(), calls=%async_computation.33 | async-start | bytes 1310720 | tf_op jit(solution)/shard_map/reduce_scatter | solution.py:43
  323.6 66.1 %all-gather.38.cloned.1.call-start = ((), (), s32[]{:S(2)}) async-start(), calls=%async_computation.24 | async-start | bytes 1310720 | tf_op jit(solution)/shard_map/all_gather | solution.py:39
  362.9 87.5 %all-gather.48.cloned.1.call-start = ((), (), s32[]{:S(2)}) async-start(), calls=%async_computation.34 | async-start | bytes 1310720 | tf_op jit(solution)/shard_map/all_gather | solution.py:49
  364.3 114.6 %reduce-scatter.27.cloned.1.call-start = ((), (), s32[]{:S(2)}) async-start(), calls=%async_computation.25 | async-start | bytes 1310720 | tf_op jit(solution)/shard_map/reduce_scatter | solution.py:43
  402.9 104.5 %reduce-scatter.37.cloned.1.call-start = ((), (), s32[]{:S(2)}) async-start(), calls=%async_computation.36 | async-start | bytes 1310720 | tf_op jit(solution)/shard_map/reduce_scatter | solution.py:53
  459.4 90.1 %all-gather.40.cloned.1.call-start = ((), (), s32[]{:S(2)}) async-start(), calls=%async_computation.26 | async-start | bytes 1310720 | tf_op jit(solution)/shard_map/all_gather | solution.py:39
  555.7 69.9 %all-gather.52.cloned.1.call-start = ((), (), s32[]{:S(2)}) async-start(), calls=%async_computation.37 | async-start | bytes 1310720 | tf_op jit(solution)/shard_map/all_gather | solution.py:49
  596.8 66.3 %reduce-scatter.39.cloned.1.call-start = ((), (), s32[]{:S(2)}) async-start(), calls=%async_computation.38 | async-start | bytes 1310720 | tf_op jit(solution)/shard_map/reduce_scatter | solution.py:53
  702.4 72.4 %all-gather.62.cloned.1.call-start = ((), (), s32[]{:S(2)}) async-start(), calls=%async_computation.46 | async-start | bytes 1310720 | tf_op jit(solution)/shard_map/all_gather | solution.py:39
  748.5 87.0 %all-gather.56.cloned.1.call-start = ((), (), s32[]{:S(2)}) async-start(), calls=%async_computation.41 | async-start | bytes 1310720 | tf_op jit(solution)/shard_map/all_gather | solution.py:49
  754.6 109.3 %reduce-scatter.47.cloned.1.call-start = ((), (), s32[]{:S(2)}) async-start(), calls=%async_computation.47 | async-start | bytes 1310720 | tf_op jit(solution)/shard_map/reduce_scatter | solution.py:43
  782.9 109.7 %reduce-scatter.43.cloned.1.call-start = ((), (), s32[]{:S(2)}) async-start(), calls=%async_computation.43 | async-start | bytes 1310720 | tf_op jit(solution)/shard_map/reduce_scatter | solution.py:53
  844.7 90.8 %all-gather.60.cloned.1.call-start = ((), (), s32[]{:S(2)}) async-start(), calls=%async_computation.44 | async-start | bytes 1310720 | tf_op jit(solution)/shard_map/all_gather | solution.py:49
  906.6 66.4 %reduce-scatter.45.cloned.1.call-start = ((), (), s32[]{:S(2)}) async-start(), calls=%async_computation.45 | async-start | bytes 1310720 | tf_op jit(solution)/shard_map/reduce_scatter | solution.py:53
  947.2 74.0 %all-gather.42.cloned.1.call-start = ((), (), s32[]{:S(2)}) async-start(), calls=%async_computation.28 | async-start | bytes 1310720 | tf_op jit(solution)/shard_map/all_gather | solution.py:39
  994.6 86.6 %all-gather.64.cloned.1.call-start = ((), (), s32[]{:S(2)}) async-start(), calls=%async_computation.48 | async-start | bytes 1310720 | tf_op jit(solution)/shard_map/all_gather | solution.py:49
  1000.8 108.9 %reduce-scatter.31.cloned.1.call-start = ((), (), s32[]{:S(2)}) async-start(), calls=%async_computation.29 | async-start | bytes 1310720 | tf_op jit(solution)/shard_map/reduce_scatter | solution.py:43
  1034.3 104.1 %reduce-scatter.49.cloned.1.call-start = ((), (), s32[]{:S(2)}) async-start(), calls=%async_computation.50 | async-start | bytes 1310720 | tf_op jit(solution)/shard_map/reduce_scatter | solution.py:53
  1088.7 91.4 %all-gather.68.cloned.1.call-start = ((), (), s32[]{:S(2)}) async-start(), calls=%async_computation.51 | async-start | bytes 1310720 | tf_op jit(solution)/shard_map/all_gather | solution.py:49
  1151.4 66.4 %reduce-scatter.51.cloned.1.call-start = ((), (), s32[]{:S(2)}) async-start(), calls=%async_computation.52 | async-start | bytes 1310720 | tf_op jit(solution)/shard_map/reduce_scatter | solution.py:53
  1192.0 63.6 %reduce-scatter.61.cloned.1.call-start = ((), (), s32[]{:S(2)}) async-start(), calls=%async_computation.60 | async-start | bytes 40960
  1199.8 81.4 %reduce-scatter.57.cloned.1.call-start = ((), (), s32[]{:S(2)}) async-start(), calls=%async_computation.55 | async-start | bytes 2621440 | tf_op jit(solution)/shard_map/reduce_scatter | solution.py:339
  1205.0 108.1 %all-gather.44.cloned.1.call-start = ((), (), s32[]{:S(2)}) async-start(), calls=%async_computation.30 | async-start | bytes 1310720 | tf_op jit(solution)/shard_map/all_gather | solution.py:39
  1229.5 120.1 %reduce-scatter.59.cloned.1.call-start = ((), (), s32[]{:S(2)}) async-start(), calls=%async_computation.56 | async-start | bytes 2621440 | tf_op jit(solution)/shard_map/reduce_scatter | solution.py:345
  1238.4 139.1 %reduce-scatter.55.cloned.1.call-start = ((), (), s32[]{:S(2)}) async-start(), calls=%async_computation.54 | async-start | bytes 655360 | tf_op jit(solution)/shard_map/reduce_scatter | solution.py:327
  1245.5 166.0 %reduce-scatter.53.cloned.1.call-start = ((), (), s32[]{:S(2)}) async-start(), calls=%async_computation.53 | async-start | bytes 1966080 | tf_op jit(solution)/shard_map/reduce_scatter | solution.py:321
  1252.1 189.0 %reduce-scatter.33.cloned.1.call-start = ((), (), s32[]{:S(2)}) async-start(), calls=%async_computation.31 | async-start | bytes 1310720 | tf_op jit(solution)/shard_map/reduce_scatter | solution.py:43
  (116 other events, 3701.3 us)
Sparse Core Ops, SparseCore 0:
  40.9 26.1 all-gather.33
  68.9 28.9 all-gather.69
  108.6 27.2 reduce-scatter.22
  137.6 33.5 all-gather.73
  172.9 35.1 all-gather.71
  210.1 29.9 all-gather.35
  246.3 25.5 reduce-scatter.24
  286.3 28.5 all-gather.45
  323.8 25.5 reduce-scatter.34
  361.0 28.6 all-gather.37
  391.9 28.2 all-gather.49
  422.1 28.2 all-gather.47
  481.6 25.7 reduce-scatter.36
  520.9 28.6 all-gather.39
  555.8 25.5 reduce-scatter.28
  596.9 28.5 all-gather.51
  665.8 28.4 all-gather.53
  746.7 28.0 all-gather.61
  776.9 28.2 all-gather.57
  807.3 28.2 all-gather.55
  866.8 25.7 reduce-scatter.42
  906.7 28.6 all-gather.59
  993.1 28.0 all-gather.41
  1023.3 28.2 all-gather.65
  1053.0 28.2 all-gather.63
  1112.6 25.7 reduce-scatter.48
  1151.5 28.6 all-gather.67
  1245.9 35.1 reduce-scatter.56
  1283.1 29.9 all-gather.43
  1316.1 33.4 reduce-scatter.58
  1380.4 31.0 reduce-scatter.52
  1413.8 27.2 reduce-scatter.32
  (9 shorter events, 226.2 us)
where the time goes:
time: 1460 us; the launch traced here: 1450 us
  waiting for transfers between devices  991 us (68%)
  blocking collectives  168 us (12%)
  matrix products  166 us (11%)
  other arithmetic  73.8 us (5%)
  local copies, waits for them, and re-layouts  24.1 us (2%)
  between operations  18.7 us (1%)
    all_gather x12, waiting for transfers between devices, full_rows(): return lax.all_gather(piece, 'tensor', axis=1, tiled=True)  273 us
    reduce_scatter x9, waiting for transfers between devices, head_sums(): lax.psum_scatter(partial_rows.astype(jnp.bfloat16), 'tensor', scatter_dim...  216 us
    all_gather x6, waiting for transfers between devices, grad_full(): return lax.all_gather(piece, 'tensor', axis=1, tiled=True)  162 us
    reduce_scatter x6, waiting for transfers between devices, back_sums(): lax.psum_scatter(partial_rows.astype(jnp.bfloat16), 'tensor', scatter_dim...  150 us
    psum x11, blocking collectives, row_totals(): return lax.psum((jnp.sum(first, axis=1), jnp.sum(second, axis=1)), 'tensor')  120 us
    all_gather x1, waiting for transfers between devices, body(): lax.all_gather(up_weight[0], 'seq', axis=0, tiled=True)  36.9 us
    all_gather x1, waiting for transfers between devices, body(): lax.all_gather(qkv_weight[0], 'seq', axis=0, tiled=True)  30.9 us
    reduce_scatter x1, waiting for transfers between devices, body(): lax.psum_scatter(totals[10].astype(jnp.bfloat16), 'seq', scatter_dimensio...  30.4 us
  transfers between devices with their start and end apart: 45, of which 44 were waited for; matrix products, arithmetic and copies ran while one was open for 10% of the time, Pallas kernels for 0%

commit v1 on v0

--- a/solution.py
+++ b/solution.py
@@ -1,3 +1,4 @@
+import functools
 import math
 import jax
 import jax.numpy as jnp
@@ -8,6 +9,40 @@
 MB = 2
 epsilon = 1e-05
 floor_value = -1e30
+
+
+def columns_feed(w_in, in_dim):
+    row_out, z, r1 = (lax.axis_size("tensor"), lax.axis_index("tensor"), w_in.shape[in_dim])
+    entries = []
+    nth = 0
+    while nth < row_out:
+        entries.append((nth, (nth + 1) % row_out))
+        nth += 1
+    xs_all = []
+    nth = 0
+    while nth < row_out:
+        xs_all.append((nth, (nth - 1) % row_out))
+        nth += 1
+    t_next = jnp.zeros((*w_in.shape[:in_dim], row_out * r1, *w_in.shape[in_dim + 1 :]), w_in.dtype)
+    t_next = lax.dynamic_update_slice_in_dim(t_next, w_in, z * r1, axis=in_dim)
+    o_now = left_arr = w_in
+    newest = row_out // 2
+    i0 = 1
+    while i0 < newest + 1:
+        o_now = lax.ppermute(o_now, perm=entries, axis_name="tensor")
+        t_next = lax.dynamic_update_slice_in_dim(
+            t_next, o_now, (z - i0) % row_out * r1, axis=in_dim
+        )
+        if i0 < row_out - newest:
+            left_arr = lax.ppermute(left_arr, axis_name="tensor", perm=xs_all)
+            t_next = lax.dynamic_update_slice_in_dim(
+                t_next, left_arr, (z + i0) % row_out * r1, axis=in_dim
+            )
+        i0 += 1
+    return t_next
+
+
+treat_stages_all = functools.partial(columns_feed, in_dim=1)
 
 
 def passed_along(shard, axis, by):
@@ -46,7 +81,7 @@
 
 
 def grad_full(piece):
-    return lax.all_gather(piece, "tensor", axis=1, tiled=True)
+    return treat_stages_all(piece)
 
 
 def back_sums(partial_rows):

time: 1460 us -> 1370 us (0.938)
  waiting for transfers between devices: 991 us -> 882 us
  starting transfers between devices: 9.04 us -> 29.9 us
  local copies, waits for them, and re-layouts: 24.1 us -> 38.8 us
    all_gather x6 -> x0, waiting for transfers between devices: 162 us -> none  [grad_full(): return lax.all_gather(piece, 'tensor', axis=1, tiled=True)]
    ppermute x0 -> x18, waiting for transfers between devices: none -> 111 us  [the longest x12 81 us: columns_feed(): o_now = lax.ppermute(o_now, perm=entries, axis_name='tensor')]
    all_gather x12, waiting for transfers between devices: 273 us -> 226 us  [full_rows(): return lax.all_gather(piece, 'tensor', axis=1, tiled=True)]
    ppermute x0 -> x18, starting transfers between devices: none -> 22.5 us  [the longest x6 14.1 us: columns_feed(): left_arr = lax.ppermute(left_arr, axis_name='tensor', perm=xs_all)]
    reduce_scatter x1, waiting for transfers between devices: 25.7 us -> 10.1 us  [body(): lax.psum_scatter(totals[4].astype(jnp.bfloat16), 'seq', scatter_dimension...]
  transfers between devices with their start and end apart: 45 -> 57, of which waited for: 44 -> 53; matrix products, arithmetic and copies ran while one was open for 10% -> 11% of each run, Pallas kernels for 0% -> 0%
where the time goes in v1:
time: 1370 us; the launch traced here: 1360 us
  waiting for transfers between devices  882 us (64%)
  blocking collectives  169 us (12%)
  matrix products  153 us (11%)
  other arithmetic  71.9 us (5%)
  local copies, waits for them, and re-layouts  38.8 us (3%)
  starting transfers between devices  29.9 us (2%)
  between operations  18.3 us (1%)
    all_gather x12, waiting for transfers between devices, full_rows(): return lax.all_gather(piece, 'tensor', axis=1, tiled=True)  226 us
    reduce_scatter x9, waiting for transfers between devices, head_sums(): lax.psum_scatter(partial_rows.astype(jnp.bfloat16), 'tensor', scatter_dim...  217 us
    reduce_scatter x6, waiting for transfers between devices, back_sums(): lax.psum_scatter(partial_rows.astype(jnp.bfloat16), 'tensor', scatter_dim...  143 us
    psum x11, blocking collectives, row_totals(): return lax.psum((jnp.sum(first, axis=1), jnp.sum(second, axis=1)), 'tensor')  121 us
    ppermute x12, waiting for transfers between devices, columns_feed(): o_now = lax.ppermute(o_now, perm=entries, axis_name='tensor')  81 us
    all_gather x1, waiting for transfers between devices, body(): lax.all_gather(up_weight[0], 'seq', axis=0, tiled=True)  36.9 us
    reduce_scatter x1, waiting for transfers between devices, body(): lax.psum_scatter(totals[10].astype(jnp.bfloat16), 'seq', scatter_dimensio...  35.9 us
    all_gather x1, waiting for transfers between devices, body(): lax.all_gather(qkv_weight[0], 'seq', axis=0, tiled=True)  30.9 us
  transfers between devices with their start and end apart: 57, of which 53 were waited for; matrix products, arithmetic and copies ran while one was open for 11% of the time, Pallas kernels for 0%

profile of v1, /device:TPU:0, one launch (start us, length us, event | category | flops | bytes accessed | tf_op | source)
XLA Modules:
  0.0 1362.1 jit_solution(904458426868130272)
XLA Ops:
  49.9 12.1 all-gather.4
  67.1 30.9 %all-gather.52.cloned.1.call-done = bf16[1,1024,4,192]{1,3,2,0:T(8,128)(2,1)} async-done(((bf16[1,256,4,192]{1,3,2,0:T(8,128)(2,1)}), bf16[1,1024,4,192]{1,3,2,0:T(8,128)(2,1)}) %all-gather.52.cloned.1.call-update) | async-done | bytes 1572880 | tf_op jit(solution)/shard_map/all_gather | solution.py:274
  109.7 26.2 %reduce-scatter.23.cloned.1.call-done = bf16[512,256]{1,0:T(8,128)(2,1)} async-done(((bf16[512,1024]{1,0:T(8,128)(2,1)}), bf16[512,256]{1,0:T(8,128)(2,1)}) %reduce-scatter.23.cloned.1.call-update) | async-done | bytes 262160 | tf_op jit(solution)/shard_map/reduce_scatter | solution.py:78
  156.5 14.8 %all-gather.56.cloned.1.call-done = bf16[1,1024,1024]{2,1,0:T(8,128)(2,1)} async-done(((bf16[1,1024,256]{2,1,0:T(8,128)(2,1)}), bf16[1,1024,1024]{2,1,0:T(8,128)(2,1)}) %all-gather.56.cloned.1.call-update) | async-done | bytes 2097168 | tf_op jit(solution)/shard_map/all_gather | solution.py:282
  171.2 36.9 %all-gather.54.cloned.1.call-done = bf16[1,1024,1024]{2,1,0:T(8,128)(2,1)} async-done(((bf16[1,256,1024]{2,1,0:T(8,128)(2,1)}), bf16[1,1024,1024]{2,1,0:T(8,128)(2,1)}) %all-gather.54.cloned.1.call-update) | async-done | bytes 2097168 | tf_op jit(solution)/shard_map/all_gather | solution.py:280
  208.1 31.9 %all-gather.30.cloned.1.call-done = bf16[512,1024]{1,0:T(8,128)(2,1)} async-done(((bf16[512,256]{1,0:T(8,128)(2,1)}), bf16[512,1024]{1,0:T(8,128)(2,1)}) %all-gather.30.cloned.1.call-update) | async-done | bytes 1048592 | tf_op jit(solution)/shard_map/all_gather | solution.py:74
  246.3 25.7 %reduce-scatter.25.cloned.1.call-done = bf16[512,256]{1,0:T(8,128)(2,1)} async-done(((bf16[512,1024]{1,0:T(8,128)(2,1)}), bf16[512,256]{1,0:T(8,128)(2,1)}) %reduce-scatter.25.cloned.1.call-update) | async-done | bytes 262160 | tf_op jit(solution)/shard_map/reduce_scatter | solution.py:78
  286.7 28.2 %all-gather.40.cloned.1.call-done = bf16[512,1024]{1,0:T(8,128)(2,1)} async-done(((bf16[512,256]{1,0:T(8,128)(2,1)}), bf16[512,1024]{1,0:T(8,128)(2,1)}) %all-gather.40.cloned.1.call-update) | async-done | bytes 1048592 | tf_op jit(solution)/shard_map/all_gather | solution.py:74
  323.9 25.5 %reduce-scatter.35.cloned.1.call-done = bf16[512,256]{1,0:T(8,128)(2,1)} async-done(((bf16[512,1024]{1,0:T(8,128)(2,1)}), bf16[512,256]{1,0:T(8,128)(2,1)}) %reduce-scatter.35.cloned.1.call-update) | async-done | bytes 262160 | tf_op jit(solution)/shard_map/reduce_scatter | solution.py:78
  364.8 25.0 %all-gather.32.cloned.1.call-done = bf16[512,1024]{1,0:T(8,128)(2,1)} async-done(((bf16[512,256]{1,0:T(8,128)(2,1)}), bf16[512,1024]{1,0:T(8,128)(2,1)}) %all-gather.32.cloned.1.call-update) | async-done | bytes 1048592 | tf_op jit(solution)/shard_map/all_gather | solution.py:74
  442.4 16.4 %reduce-scatter.27.cloned.1.call-done = bf16[512,256]{1,0:T(8,128)(2,1)} async-done(((bf16[512,1024]{1,0:T(8,128)(2,1)}), bf16[512,256]{1,0:T(8,128)(2,1)}) %reduce-scatter.27.cloned.1.call-update) | async-done | bytes 262160 | tf_op jit(solution)/shard_map/reduce_scatter | solution.py:78
  458.8 28.1 %reduce-scatter.37.cloned.1.call-done = bf16[512,256]{1,0:T(8,128)(2,1)} async-done(((bf16[512,1024]{1,0:T(8,128)(2,1)}), bf16[512,256]{1,0:T(8,128)(2,1)}) %reduce-scatter.37.cloned.1.call-update) | async-done | bytes 262160 | tf_op jit(solution)/shard_map/reduce_scatter | solution.py:88
  500.3 28.8 %all-gather.34.cloned.1.call-done = bf16[512,1024]{1,0:T(8,128)(2,1)} async-done(((bf16[512,256]{1,0:T(8,128)(2,1)}), bf16[512,1024]{1,0:T(8,128)(2,1)}) %all-gather.34.cloned.1.call-update) | async-done | bytes 1048592 | tf_op jit(solution)/shard_map/all_gather | solution.py:74
  535.2 25.7 %reduce-scatter.29.cloned.1.call-done = bf16[512,256]{1,0:T(8,128)(2,1)} async-done(((bf16[512,1024]{1,0:T(8,128)(2,1)}), bf16[512,256]{1,0:T(8,128)(2,1)}) %reduce-scatter.29.cloned.1.call-update) | async-done | bytes 262160 | tf_op jit(solution)/shard_map/reduce_scatter | solution.py:78
  604.2 25.4 %reduce-scatter.39.cloned.1.call-done = bf16[512,256]{1,0:T(8,128)(2,1)} async-done(((bf16[512,1024]{1,0:T(8,128)(2,1)}), bf16[512,256]{1,0:T(8,128)(2,1)}) %reduce-scatter.39.cloned.1.call-update) | async-done | bytes 262160 | tf_op jit(solution)/shard_map/reduce_scatter | solution.py:88
  632.5 28.3 %all-gather.44.cloned.1.call-done = bf16[512,1024]{1,0:T(8,128)(2,1)} async-done(((bf16[512,256]{1,0:T(8,128)(2,1)}), bf16[512,1024]{1,0:T(8,128)(2,1)}) %all-gather.44.cloned.1.call-update) | async-done | bytes 1048592 | tf_op jit(solution)/shard_map/all_gather | solution.py:74
  669.6 25.7 %reduce-scatter.41.cloned.1.call-done = bf16[512,256]{1,0:T(8,128)(2,1)} async-done(((bf16[512,1024]{1,0:T(8,128)(2,1)}), bf16[512,256]{1,0:T(8,128)(2,1)}) %reduce-scatter.41.cloned.1.call-update) | async-done | bytes 262160 | tf_op jit(solution)/shard_map/reduce_scatter | solution.py:78
  696.5 16.8 %all-reduce.17 = (f32[512]{0:T(512)S(1)}, f32[512]{0:T(512)S(1)}, f32[512]{0:T(512)S(1)}, f32[512]{0:T(512)S(1)}, f32[512]{0:T(512)S(1)}, /*index=5*/f32[512]{0:T(512)}) all-reduce(f32[512]{0:T(512)S(1)} %get-tuple-element.31, f32[512]{0:T(512)S(1)} %get-tuple-element.30, ...), channel_id=1, replica_groups=mesh['section'=2,'seq'=4,'tensor'=4] {'tensor'}, use_global_device_ids=true, to_apply=%region_66.67 | all-reduce | flops 3072 | bytes 24576 | tf_op jit(solution)/shard_map/psum | solution.py:55
  772.0 17.5 %all-gather.48.cloned.1.call-done = bf16[512,1024]{1,0:T(8,128)(2,1)} async-done(((bf16[512,256]{1,0:T(8,128)(2,1)}), bf16[512,1024]{1,0:T(8,128)(2,1)}) %all-gather.48.cloned.1.call-update) | async-done | bytes 1048592 | tf_op jit(solution)/shard_map/all_gather | solution.py:74
  797.5 19.9 %reduce-scatter.43.cloned.1.call-done = bf16[512,256]{1,0:T(8,128)(2,1)} async-done(((bf16[512,1024]{1,0:T(8,128)(2,1)}), bf16[512,256]{1,0:T(8,128)(2,1)}) %reduce-scatter.43.cloned.1.call-update) | async-done | bytes 262160 | tf_op jit(solution)/shard_map/reduce_scatter | solution.py:88
  817.4 28.1 %reduce-scatter.47.cloned.1.call-done = bf16[512,256]{1,0:T(8,128)(2,1)} async-done(((bf16[512,1024]{1,0:T(8,128)(2,1)}), bf16[512,256]{1,0:T(8,128)(2,1)}) %reduce-scatter.47.cloned.1.call-update) | async-done | bytes 262160 | tf_op jit(solution)/shard_map/reduce_scatter | solution.py:78
  887.5 25.5 %reduce-scatter.45.cloned.1.call-done = bf16[512,256]{1,0:T(8,128)(2,1)} async-done(((bf16[512,1024]{1,0:T(8,128)(2,1)}), bf16[512,256]{1,0:T(8,128)(2,1)}) %reduce-scatter.45.cloned.1.call-update) | async-done | bytes 262160 | tf_op jit(solution)/shard_map/reduce_scatter | solution.py:88
  914.9 16.8 %all-reduce.15 = (f32[512]{0:T(512)}, f32[512]{0:T(512)}, f32[512]{0:T(512)S(1)}, f32[512]{0:T(512)S(1)}, f32[512]{0:T(512)}, /*index=5*/f32[512]{0:T(512)S(1)}) all-reduce(f32[512]{0:T(512)S(1)} %get-tuple-element.147, f32[512]{0:T(512)S(1)} %get-tuple-element.148, ...), channel_id=1, replica_groups=mesh['section'=2,'seq'=4,'tensor'=4] {'tensor'}, use_global_device_ids=true, to_apply=%region_27.28 | all-reduce | flops 3072 | bytes 24576 | tf_op jit(solution)/shard_map/psum | solution.py:55
  941.6 24.9 %all-gather.36.cloned.1.call-done = bf16[512,1024]{1,0:T(8,128)(2,1)} async-done(((bf16[512,256]{1,0:T(8,128)(2,1)}), bf16[512,1024]{1,0:T(8,128)(2,1)}) %all-gather.36.cloned.1.call-update) | async-done | bytes 1048592 | tf_op jit(solution)/shard_map/all_gather | solution.py:74
  1019.1 16.4 %reduce-scatter.31.cloned.1.call-done = bf16[512,256]{1,0:T(8,128)(2,1)} async-done(((bf16[512,1024]{1,0:T(8,128)(2,1)}), bf16[512,256]{1,0:T(8,128)(2,1)}) %reduce-scatter.31.cloned.1.call-update) | async-done | bytes 262160 | tf_op jit(solution)/shard_map/reduce_scatter | solution.py:78
  1035.5 28.0 %reduce-scatter.49.cloned.1.call-done = bf16[512,256]{1,0:T(8,128)(2,1)} async-done(((bf16[512,1024]{1,0:T(8,128)(2,1)}), bf16[512,256]{1,0:T(8,128)(2,1)}) %reduce-scatter.49.cloned.1.call-update) | async-done | bytes 262160 | tf_op jit(solution)/shard_map/reduce_scatter | solution.py:88
  1112.9 16.1 %reduce-scatter.51.cloned.1.call-done = bf16[512,256]{1,0:T(8,128)(2,1)} async-done(((bf16[512,1024]{1,0:T(8,128)(2,1)}), bf16[512,256]{1,0:T(8,128)(2,1)}) %reduce-scatter.51.cloned.1.call-update) | async-done | bytes 262160 | tf_op jit(solution)/shard_map/reduce_scatter | solution.py:88
  1184.4 30.5 %all-gather.38.cloned.1.call-done = bf16[512,1024]{1,0:T(8,128)(2,1)} async-done(((bf16[512,256]{1,0:T(8,128)(2,1)}), bf16[512,1024]{1,0:T(8,128)(2,1)}) %all-gather.38.cloned.1.call-update) | async-done | bytes 1048592 | tf_op jit(solution)/shard_map/all_gather | solution.py:74
  1221.0 30.4 %reduce-scatter.57.cloned.1.call-done = bf16[256,1024]{1,0:T(8,128)(2,1)} async-done(((bf16[1024,1024]{1,0:T(8,128)(2,1)}), bf16[256,1024]{1,0:T(8,128)(2,1)}) %reduce-scatter.57.cloned.1.call-update) | async-done | bytes 524304 | tf_op jit(solution)/shard_map/reduce_scatter | solution.py:374
  1253.5 35.9 %reduce-scatter.59.cloned.1.call-done = bf16[1024,256]{1,0:T(8,128)(2,1)} async-done(((bf16[1024,1024]{1,0:T(8,128)(2,1)}), bf16[1024,256]{1,0:T(8,128)(2,1)}) %reduce-scatter.59.cloned.1.call-update) | async-done | bytes 524304 | tf_op jit(solution)/shard_map/reduce_scatter | solution.py:380
  1306.2 17.3 %reduce-scatter.53.cloned.1.call-done = bf16[256,4,192]{0,2,1:T(8,128)(2,1)} async-done(((bf16[1024,4,192]{0,2,1:T(8,128)(2,1)}), bf16[256,4,192]{0,2,1:T(8,128)(2,1)}) %reduce-scatter.53.cloned.1.call-update) | async-done | bytes 393232 | tf_op jit(solution)/shard_map/reduce_scatter | solution.py:356
  1325.5 27.7 %reduce-scatter.33.cloned.1.call-done = bf16[512,256]{1,0:T(8,128)(2,1)} async-done(((bf16[512,1024]{1,0:T(8,128)(2,1)}), bf16[512,256]{1,0:T(8,128)(2,1)}) %reduce-scatter.33.cloned.1.call-update) | async-done | bytes 262160 | tf_op jit(solution)/shard_map/reduce_scatter | solution.py:78
  (545 shorter events, 556.5 us)
Async XLA Ops:
  41.5 94.4 %reduce-scatter.23.cloned.1.call-start = ((), (), s32[]{:S(2)}) async-start(), calls=%async_computation.21 | async-start | bytes 1310720 | tf_op jit(solution)/shard_map/reduce_scatter | solution.py:78
  108.5 62.7 %all-gather.56.cloned.1.call-start = ((), (), s32[]{:S(2)}) async-start(), calls=%async_computation.53 | async-start | bytes 2621440 | tf_op jit(solution)/shard_map/all_gather | solution.py:282
  109.1 99.1 %all-gather.54.cloned.1.call-start = ((), (), s32[]{:S(2)}) async-start(), calls=%async_computation.52 | async-start | bytes 2621440 | tf_op jit(solution)/shard_map/all_gather | solution.py:280
  109.7 130.4 %all-gather.30.cloned.1.call-start = ((), (), s32[]{:S(2)}) async-start(), calls=%async_computation.22 | async-start | bytes 1310720 | tf_op jit(solution)/shard_map/all_gather | solution.py:74
  148.3 123.6 %reduce-scatter.25.cloned.1.call-start = ((), (), s32[]{:S(2)}) async-start(), calls=%async_computation.23 | async-start | bytes 1310720 | tf_op jit(solution)/shard_map/reduce_scatter | solution.py:78
  246.2 68.7 %all-gather.40.cloned.1.call-start = ((), (), s32[]{:S(2)}) async-start(), calls=%async_computation.32 | async-start | bytes 1310720 | tf_op jit(solution)/shard_map/all_gather | solution.py:74
  286.2 63.1 %reduce-scatter.35.cloned.1.call-start = ((), (), s32[]{:S(2)}) async-start(), calls=%async_computation.33 | async-start | bytes 1310720 | tf_op jit(solution)/shard_map/reduce_scatter | solution.py:78
  323.6 66.1 %all-gather.32.cloned.1.call-start = ((), (), s32[]{:S(2)}) async-start(), calls=%async_computation.24 | async-start | bytes 1310720 | tf_op jit(solution)/shard_map/all_gather | solution.py:74
  360.9 69.7 %all-gather.42.cloned.1.call-start = ((), (), s32[]{:S(2)}) async-start(), calls=%async_computation.34 | async-start | bytes 1310720 | tf_op jit(solution)/shard_map/all_gather | solution.py:74
  364.5 94.3 %reduce-scatter.27.cloned.1.call-start = ((), (), s32[]{:S(2)}) async-start(), calls=%async_computation.25 | async-start | bytes 1310720 | tf_op jit(solution)/shard_map/reduce_scatter | solution.py:78
  402.9 84.0 %reduce-scatter.37.cloned.1.call-start = ((), (), s32[]{:S(2)}) async-start(), calls=%async_computation.35 | async-start | bytes 1310720 | tf_op jit(solution)/shard_map/reduce_scatter | solution.py:88
  442.3 86.7 %all-gather.34.cloned.1.call-start = ((), (), s32[]{:S(2)}) async-start(), calls=%async_computation.26 | async-start | bytes 1310720 | tf_op jit(solution)/shard_map/all_gather | solution.py:74
  500.2 60.6 %reduce-scatter.29.cloned.1.call-start = ((), (), s32[]{:S(2)}) async-start(), calls=%async_computation.27 | async-start | bytes 1310720 | tf_op jit(solution)/shard_map/reduce_scatter | solution.py:78
  535.1 94.5 %reduce-scatter.39.cloned.1.call-start = ((), (), s32[]{:S(2)}) async-start(), calls=%async_computation.36 | async-start | bytes 1310720 | tf_op jit(solution)/shard_map/reduce_scatter | solution.py:88
  632.3 63.0 %reduce-scatter.41.cloned.1.call-start = ((), (), s32[]{:S(2)}) async-start(), calls=%async_computation.38 | async-start | bytes 1310720 | tf_op jit(solution)/shard_map/reduce_scatter | solution.py:78
  669.6 90.5 %all-gather.46.cloned.1.call-start = ((), (), s32[]{:S(2)}) async-start(), calls=%async_computation.39 | async-start | bytes 1310720 | tf_op jit(solution)/shard_map/all_gather | solution.py:74
  715.2 74.3 %all-gather.48.cloned.1.call-start = ((), (), s32[]{:S(2)}) async-start(), calls=%async_computation.42 | async-start | bytes 1310720 | tf_op jit(solution)/shard_map/all_gather | solution.py:74
  726.5 90.9 %reduce-scatter.43.cloned.1.call-start = ((), (), s32[]{:S(2)}) async-start(), calls=%async_computation.40 | async-start | bytes 1310720 | tf_op jit(solution)/shard_map/reduce_scatter | solution.py:88
  771.8 73.8 %reduce-scatter.47.cloned.1.call-start = ((), (), s32[]{:S(2)}) async-start(), calls=%async_computation.43 | async-start | bytes 1310720 | tf_op jit(solution)/shard_map/reduce_scatter | solution.py:78
  797.5 115.5 %reduce-scatter.45.cloned.1.call-start = ((), (), s32[]{:S(2)}) async-start(), calls=%async_computation.41 | async-start | bytes 1310720 | tf_op jit(solution)/shard_map/reduce_scatter | solution.py:88
  887.5 79.0 %all-gather.36.cloned.1.call-start = ((), (), s32[]{:S(2)}) async-start(), calls=%async_computation.28 | async-start | bytes 1310720 | tf_op jit(solution)/shard_map/all_gather | solution.py:74
  933.4 74.4 %all-gather.50.cloned.1.call-start = ((), (), s32[]{:S(2)}) async-start(), calls=%async_computation.44 | async-start | bytes 1310720 | tf_op jit(solution)/shard_map/all_gather | solution.py:74
  939.1 96.4 %reduce-scatter.31.cloned.1.call-start = ((), (), s32[]{:S(2)}) async-start(), calls=%async_computation.29 | async-start | bytes 1310720 | tf_op jit(solution)/shard_map/reduce_scatter | solution.py:78
  979.7 83.8 %reduce-scatter.49.cloned.1.call-start = ((), (), s32[]{:S(2)}) async-start(), calls=%async_computation.45 | async-start | bytes 1310720 | tf_op jit(solution)/shard_map/reduce_scatter | solution.py:88
  1019.0 110.0 %reduce-scatter.51.cloned.1.call-start = ((), (), s32[]{:S(2)}) async-start(), calls=%async_computation.46 | async-start | bytes 1310720 | tf_op jit(solution)/shard_map/reduce_scatter | solution.py:88
  1103.4 67.8 %reduce-scatter.61.cloned.1.call-start = ((), (), s32[]{:S(2)}) async-start(), calls=%async_computation.54 | async-start | bytes 40960
  1109.5 73.3 %reduce-scatter.55.cloned.1.call-start = ((), (), s32[]{:S(2)}) async-start(), calls=%async_computation.48 | async-start | bytes 655360 | tf_op jit(solution)/shard_map/reduce_scatter | solution.py:362
  1112.7 102.2 %all-gather.38.cloned.1.call-start = ((), (), s32[]{:S(2)}) async-start(), calls=%async_computation.30 | async-start | bytes 1310720 | tf_op jit(solution)/shard_map/all_gather | solution.py:74
  1141.3 110.1 %reduce-scatter.57.cloned.1.call-start = ((), (), s32[]{:S(2)}) async-start(), calls=%async_computation.49 | async-start | bytes 2621440 | tf_op jit(solution)/shard_map/reduce_scatter | solution.py:374
  1148.9 140.6 %reduce-scatter.59.cloned.1.call-start = ((), (), s32[]{:S(2)}) async-start(), calls=%async_computation.50 | async-start | bytes 2621440 | tf_op jit(solution)/shard_map/reduce_scatter | solution.py:380
  1160.4 163.2 %reduce-scatter.53.cloned.1.call-start = ((), (), s32[]{:S(2)}) async-start(), calls=%async_computation.47 | async-start | bytes 1966080 | tf_op jit(solution)/shard_map/reduce_scatter | solution.py:356
  1168.9 184.3 %reduce-scatter.33.cloned.1.call-start = ((), (), s32[]{:S(2)}) async-start(), calls=%async_computation.31 | async-start | bytes 1310720 | tf_op jit(solution)/shard_map/reduce_scatter | solution.py:78
  (120 other events, 2620.2 us)
Sparse Core Ops, SparseCore 0:
  40.9 26.1 all-gather.27
  68.9 28.9 all-gather.51
  108.6 27.2 reduce-scatter.22
  137.6 33.5 all-gather.55
  172.9 35.1 all-gather.53
  210.1 29.9 all-gather.29
  246.3 25.5 reduce-scatter.24
  286.3 28.5 all-gather.39
  323.7 25.5 reduce-scatter.34
  361.0 28.6 all-gather.31
  391.9 38.6 all-gather.41
  433.3 25.4 reduce-scatter.26
  461.1 25.7 reduce-scatter.36
  500.3 28.6 all-gather.33
  535.2 25.5 reduce-scatter.28
  632.4 28.4 all-gather.43
  669.7 25.5 reduce-scatter.40
  715.4 43.2 all-gather.45
  760.6 28.8 all-gather.47
  791.8 25.5 reduce-scatter.42
  819.7 25.7 reduce-scatter.46
  887.6 25.3 reduce-scatter.44
  933.5 32.9 all-gather.35
  968.6 39.1 all-gather.49
  1010.0 25.4 reduce-scatter.30
  1037.6 25.7 reduce-scatter.48
  1103.6 25.3 reduce-scatter.50
  1184.9 29.9 all-gather.37
  1217.9 33.4 reduce-scatter.56
  1254.2 35.1 reduce-scatter.58
  1292.4 31.1 reduce-scatter.52
  1325.9 27.2 reduce-scatter.32
  (3 shorter events, 72.9 us)
